TPU v7x, 32 devices: a whole 2x2x4 slice. The times are simulated.
32 devices in a mesh: ia: 4 (over y, core), ja: 2 (over x), ka: 4 (over z).
Axes of the slice: x: 2, y: 2, z: 4, core: 2. Of those that a mesh axis runs over, the one named last changes fastest.
Arguments:
- block_coords: int32 [4, 2, 4, 4, 3], P('ia', 'ja', 'ka'), may hold values from 0 to 3, as said below
- live_blocks: int32 [4, 2, 4], P('ia', 'ja', 'ka'), may hold values from 1 to 4, as said below
- counts: int32 [4, 2, 4, 4, 64, 4096], P('ia', 'ja', 'ka'), may hold values from 0 to 7
- factor_a: float32 [1024, 256], P(('ia', 'ja', 'ka')), may hold values from 0.3 to 9.6
- factor_b: float32 [512, 256], P(('ja', 'ka')), may hold values from 0.05 to 8
- factor_c: float32 [1024, 256], P('ka', 'ia'), may hold values from 0.05 to 8
Outputs:
- factor_new: float32 [1024, 256], P(('ia', 'ja', 'ka'))
Inputs may be any that keep to these rules, and one draw needn't show every extreme that they name: `block_coords`: a device's slots name distinct blocks; slot 0 is always live, and every mode-1 block of the slab has a live block on some device. `live_blocks`: on some device all 4 slots are live.
All inputs are finite; a program needn't handle non-finite values.
Results may differ from a plain program's by a relative error of at most 0.00061.
Values may be sent and summed in bfloat16 or wider, within the bound.
A program may use at most 64 MiB of HBM per device.

v0:
```python
import jax
import jax.numpy as jnp
from jax import lax
from jax.sharding import PartitionSpec as P

R = 256
BS = 64
RB1 = 4
RB2 = 4
RB3 = 4
SLOTS = 4


def make_panel(rows_b, rows_c, index_j, index_k):
    piece_b = lax.dynamic_slice_in_dim(rows_b, index_j * BS, BS, 0)
    piece_c = lax.dynamic_slice_in_dim(rows_c, index_k * BS, BS, 0)
    return (piece_b[:, None, :] * piece_c[None, :, :]).reshape(BS * BS, R).astype(jnp.bfloat16)


def add_block(phi, factor_low, panel, index_i, weight, block_counts):
    block_a = lax.dynamic_slice_in_dim(factor_low, index_i * BS, BS, 0)
    model = lax.dot_general(
        block_a, panel, (((1,), (1,)), ((), ())), preferred_element_type=jnp.float32
    )
    ratio = (block_counts.astype(jnp.float32) / model).astype(jnp.bfloat16)
    part = jnp.dot(ratio, panel, preferred_element_type=jnp.float32) * weight
    old = lax.dynamic_slice_in_dim(phi, index_i * BS, BS, 0)
    return lax.dynamic_update_slice_in_dim(phi, old + part, index_i * BS, 0)


def local(block_coords, live_blocks, counts, factor_a, factor_b, factor_c):
    coords = block_coords.reshape(SLOTS, 3)
    local_counts = counts.reshape(SLOTS, BS, BS * BS)
    weights = (jnp.arange(SLOTS, dtype=jnp.int32) < live_blocks.reshape(())).astype(jnp.float32)
    rows_b = lax.all_gather(factor_b, "ka", axis=0, tiled=True)
    rows_c = lax.all_gather(factor_c, "ia", axis=1, tiled=True)
    sums_b = rows_b.reshape(RB2, BS, R).sum(axis=1)
    sums_c = rows_c.reshape(RB3, BS, R).sum(axis=1)
    pick_j = (coords[:, 1:2] == jnp.arange(RB2, dtype=jnp.int32)[None, :]).astype(jnp.float32)
    pick_k = (coords[:, 2:3] == jnp.arange(RB3, dtype=jnp.int32)[None, :]).astype(jnp.float32)
    masses = jnp.dot(pick_j, sums_b, precision=lax.Precision.HIGHEST) * jnp.dot(
        pick_k, sums_c, precision=lax.Precision.HIGHEST
    )
    pick_i = (coords[:, 0:1] == jnp.arange(RB1, dtype=jnp.int32)[None, :]).astype(
        jnp.float32
    ) * weights[:, None]
    mass_part = lax.dot_general(
        pick_i, masses, (((0,), (0,)), ((), ())), precision=lax.Precision.HIGHEST
    )
    mass = lax.psum(mass_part, ("ja", "ka"))
    mass_rows = jnp.broadcast_to(mass[:, None, :], (RB1, BS, R)).reshape(RB1 * BS, R)
    owned = factor_a.shape[0]
    first_row = lax.axis_index(("ja", "ka")) * owned
    my_mass = lax.dynamic_slice_in_dim(mass_rows, first_row, owned, 0)
    empty = jnp.zeros((RB1 * BS, R), jnp.float32)

    def accumulate(factor_low):

        def step(phi, item):
            index_i, index_j, index_k, weight, block_counts = item
            panel = make_panel(rows_b, rows_c, index_j, index_k)
            return (add_block(phi, factor_low, panel, index_i, weight, block_counts), None)

        phi, _ = lax.scan(
            step, empty, (coords[:, 0], coords[:, 1], coords[:, 2], weights, local_counts)
        )
        return phi

    whole = lax.all_gather(factor_a, ("ja", "ka"), axis=0, tiled=True)
    phi = accumulate(whole.astype(jnp.bfloat16))
    totals = lax.psum(phi, ("ja", "ka"))
    updated = whole * totals / mass_rows
    phi = accumulate(updated.astype(jnp.bfloat16))
    mine = lax.psum_scatter(phi, ("ja", "ka"), scatter_dimension=0, tiled=True)
    return lax.dynamic_slice_in_dim(updated, first_row, owned, 0) * mine / my_mass


def solution(mesh):
    placed = (
        P("ia", "ja", "ka", None, None),
        P("ia", "ja", "ka"),
        P("ia", "ja", "ka", None, None, None),
        P(("ia", "ja", "ka"), None),
        P(("ja", "ka"), None),
        P("ka", "ia"),
    )
    return jax.shard_map(
        local, mesh=mesh, in_specs=placed, out_specs=P(("ia", "ja", "ka"), None), check_vma=False
    )
```

profile of v0, /device:TPU:0, one launch (start us, length us, event | category | flops | bytes accessed | tf_op | source)
XLA Modules:
  0.0 275.6 jit_solution(7233616077265290646)
XLA Ops:
  6.5 0.8 copy.14
  7.5 7.5 %all_gather.11 = f32[256,256]{0,1:T(8,128)S(1)} all-gather(f32[256,64]{0,1:T(8,128)} %param.15), channel_id=1, replica_groups=mesh['ia'=4,'ja'=2,'ka'=4] {'ia'}, dimensions={1}, use_global_device_ids=true | all-gather | bytes 327680 | tf_op jit(solution)/shard_map/all_gather | solution.py:36
  15.1 14.3 %all_gather.10 = f32[256,256]{1,0:T(8,128)S(1)} all-gather(f32[64,256]{1,0:T(8,128)} %param.14), channel_id=1, replica_groups=mesh['ia'=4,'ja'=2,'ka'=4] {'ka'}, dimensions={0}, use_global_device_ids=true | all-gather | bytes 327680 | tf_op jit(solution)/shard_map/all_gather | solution.py:35
  30.1 31.8 %all_gather.9 = f32[256,256]{1,0:T(8,128)S(1)} all-gather(f32[32,256]{1,0:T(8,128)} %param.13), channel_id=1, replica_groups=mesh['ia'=4,'ja'=2,'ka'=4] {'ja','ka'}, dimensions={0}, use_global_device_ids=true | all-gather | bytes 294912 | tf_op jit(solution)/shard_map/all_gather | solution.py:69
  62.0 34.4 %while.20 = (s32[]{:T(128)}, f32[256,256]{1,0:T(8,128)S(1)}, s32[4]{0:T(128)S(1)}, s32[4,64,4096]{2,1,0:T(8,128)}, bf16[256,256]{1,0:T(8,128)(2,1)S(1)}, /*index...) while((s32[]{:T(128)}, f32[256,256]{1,0:T(8,128)S(1)}, ...), condition=%wide.region_1.0_spmd, body=%wide.region_0.0_spmd.sunk | while | flops 271351808 | bytes 7899463 | solution.py:64
  63.3 0.7 dynamic_slice.109
  64.7 0.7 multiply_convert_fusion.4
  65.4 0.7 dynamic_slice.107
  66.8 0.7 dynamic_slice.110
  67.5 3.1 %fusion.52 = f32[256,256]{1,0:T(8,128)S(1)} fusion(f32[256,256]{1,0:T(8,128)S(1)} %get-tuple-element.345, s32[]{:T(128)S(6)} %select_n.33, bf16[4096,256]{1,0:T(8,128)(2,1)S(1)} %bitcast.70, s32[4,64,4096]{2,1,0:T(8,128)} %get-tuple-element.361, s32[]{:T(128)} %get-tuple-element.344, f32[]{:T(128)} %bitcast.60, ...), kind=kOutput, calls=%fused_computation.6.clone.1 | convolution fusion | flops 269254656 | bytes 5408768 | tf_op jit(solution)/shard_map/while/body/eval_jaxpr/dot_general | solution.py:26
  71.9 0.7 dynamic_slice.109
  73.3 0.7 multiply_convert_fusion.4
  74.0 0.7 dynamic_slice.107
  75.4 0.7 dynamic_slice.110
  76.1 3.1 %fusion.52 = f32[256,256]{1,0:T(8,128)S(1)} fusion(f32[256,256]{1,0:T(8,128)S(1)} %get-tuple-element.345, s32[]{:T(128)S(6)} %select_n.33, bf16[4096,256]{1,0:T(8,128)(2,1)S(1)} %bitcast.70, s32[4,64,4096]{2,1,0:T(8,128)} %get-tuple-element.361, s32[]{:T(128)} %get-tuple-element.344, f32[]{:T(128)} %bitcast.60, ...), kind=kOutput, calls=%fused_computation.6.clone.1 | convolution fusion | flops 269254656 | bytes 5408768 | tf_op jit(solution)/shard_map/while/body/eval_jaxpr/dot_general | solution.py:26
  80.5 0.7 dynamic_slice.109
  81.9 0.7 multiply_convert_fusion.4
  82.6 0.7 dynamic_slice.107
  84.0 0.7 dynamic_slice.110
  84.7 3.1 %fusion.52 = f32[256,256]{1,0:T(8,128)S(1)} fusion(f32[256,256]{1,0:T(8,128)S(1)} %get-tuple-element.345, s32[]{:T(128)S(6)} %select_n.33, bf16[4096,256]{1,0:T(8,128)(2,1)S(1)} %bitcast.70, s32[4,64,4096]{2,1,0:T(8,128)} %get-tuple-element.361, s32[]{:T(128)} %get-tuple-element.344, f32[]{:T(128)} %bitcast.60, ...), kind=kOutput, calls=%fused_computation.6.clone.1 | convolution fusion | flops 269254656 | bytes 5408768 | tf_op jit(solution)/shard_map/while/body/eval_jaxpr/dot_general | solution.py:26
  89.2 0.7 dynamic_slice.109
  90.5 0.7 multiply_convert_fusion.4
  92.6 0.7 dynamic_slice.110
  93.3 3.1 %fusion.52 = f32[256,256]{1,0:T(8,128)S(1)} fusion(f32[256,256]{1,0:T(8,128)S(1)} %get-tuple-element.345, s32[]{:T(128)S(6)} %select_n.33, bf16[4096,256]{1,0:T(8,128)(2,1)S(1)} %bitcast.70, s32[4,64,4096]{2,1,0:T(8,128)} %get-tuple-element.361, s32[]{:T(128)} %get-tuple-element.344, f32[]{:T(128)} %bitcast.60, ...), kind=kOutput, calls=%fused_computation.6.clone.1 | convolution fusion | flops 269254656 | bytes 5408768 | tf_op jit(solution)/shard_map/while/body/eval_jaxpr/dot_general | solution.py:26
  96.4 0.7 copy-done.1
  97.9 21.7 %psum.15 = f32[4,256]{1,0:T(4,128)S(1)} all-reduce(f32[4,256]{1,0:T(4,128)S(1)} %fusion.24), channel_id=1, replica_groups=mesh['ia'=4,'ja'=2,'ka'=4] {'ja','ka'}, use_global_device_ids=true, to_apply=%region_5.6 | all-reduce | flops 1024 | bytes 8192 | tf_op jit(solution)/shard_map/psum | solution.py:50
  119.5 49.9 %all-reduce.2.cloned.1.call-done = f32[256,256]{1,0:T(8,128)} async-done(((f32[256,256]{1,0:T(8,128)}), f32[256,256]{1,0:T(8,128)}) %all-reduce.2.cloned.1.call-update) | async-done | bytes 262160 | tf_op jit(solution)/shard_map/psum | solution.py:71
  169.4 1.0 fusion.33
  170.5 34.4 %while.21 = (s32[]{:T(128)}, f32[256,256]{1,0:T(8,128)S(1)}, s32[4]{0:T(128)S(1)}, s32[4,64,4096]{2,1,0:T(8,128)}, bf16[256,256]{1,0:T(8,128)(2,1)S(1)}, /*index...) while((s32[]{:T(128)}, f32[256,256]{1,0:T(8,128)S(1)}, ...), condition=%wide.region_7.8_spmd, body=%wide.region_6.7_spmd.sunk | while | flops 271351808 | bytes 7899463 | solution.py:64
  171.8 0.7 dynamic_slice.117
  173.2 0.7 multiply_convert_fusion.5
  173.9 0.7 dynamic_slice.115
  175.3 0.7 dynamic_slice.118
  176.0 3.1 %fusion.56 = f32[256,256]{1,0:T(8,128)S(1)} fusion(f32[256,256]{1,0:T(8,128)S(1)} %get-tuple-element.387, s32[]{:T(128)S(6)} %select_n.36, bf16[4096,256]{1,0:T(8,128)(2,1)S(1)} %bitcast.71, s32[4,64,4096]{2,1,0:T(8,128)} %get-tuple-element.403, s32[]{:T(128)} %get-tuple-element.386, f32[]{:T(128)} %bitcast.68, ...), kind=kOutput, calls=%fused_computation.20.clone.1 | convolution fusion | flops 269254656 | bytes 5408768 | tf_op jit(solution)/shard_map/while/body/eval_jaxpr/dot_general | solution.py:26
  180.4 0.7 dynamic_slice.117
  181.8 0.7 multiply_convert_fusion.5
  182.5 0.7 dynamic_slice.115
  183.9 0.7 dynamic_slice.118
  184.6 3.1 %fusion.56 = f32[256,256]{1,0:T(8,128)S(1)} fusion(f32[256,256]{1,0:T(8,128)S(1)} %get-tuple-element.387, s32[]{:T(128)S(6)} %select_n.36, bf16[4096,256]{1,0:T(8,128)(2,1)S(1)} %bitcast.71, s32[4,64,4096]{2,1,0:T(8,128)} %get-tuple-element.403, s32[]{:T(128)} %get-tuple-element.386, f32[]{:T(128)} %bitcast.68, ...), kind=kOutput, calls=%fused_computation.20.clone.1 | convolution fusion | flops 269254656 | bytes 5408768 | tf_op jit(solution)/shard_map/while/body/eval_jaxpr/dot_general | solution.py:26
  189.0 0.7 dynamic_slice.117
  190.4 0.7 multiply_convert_fusion.5
  191.1 0.7 dynamic_slice.115
  193.2 3.1 %fusion.56 = f32[256,256]{1,0:T(8,128)S(1)} fusion(f32[256,256]{1,0:T(8,128)S(1)} %get-tuple-element.387, s32[]{:T(128)S(6)} %select_n.36, bf16[4096,256]{1,0:T(8,128)(2,1)S(1)} %bitcast.71, s32[4,64,4096]{2,1,0:T(8,128)} %get-tuple-element.403, s32[]{:T(128)} %get-tuple-element.386, f32[]{:T(128)} %bitcast.68, ...), kind=kOutput, calls=%fused_computation.20.clone.1 | convolution fusion | flops 269254656 | bytes 5408768 | tf_op jit(solution)/shard_map/while/body/eval_jaxpr/dot_general | solution.py:26
  199.0 0.7 multiply_convert_fusion.5
  201.8 3.1 %fusion.56 = f32[256,256]{1,0:T(8,128)S(1)} fusion(f32[256,256]{1,0:T(8,128)S(1)} %get-tuple-element.387, s32[]{:T(128)S(6)} %select_n.36, bf16[4096,256]{1,0:T(8,128)(2,1)S(1)} %bitcast.71, s32[4,64,4096]{2,1,0:T(8,128)} %get-tuple-element.403, s32[]{:T(128)} %get-tuple-element.386, f32[]{:T(128)} %bitcast.68, ...), kind=kOutput, calls=%fused_computation.20.clone.1 | convolution fusion | flops 269254656 | bytes 5408768 | tf_op jit(solution)/shard_map/while/body/eval_jaxpr/dot_general | solution.py:26
  204.9 0.7 copy-done
  205.6 61.8 %reduce-scatter.2.cloned.1.call-done = f32[32,256]{1,0:T(8,128)} async-done(((f32[256,256]{1,0:T(8,128)}), f32[32,256]{1,0:T(8,128)}) %reduce-scatter.2.cloned.1.call-update) | async-done | bytes 32784 | tf_op jit(solution)/shard_map/reduce_scatter | solution.py:74
  267.4 1.4 dynamic-slice_divide_fusion
  (39 shorter events, 10.0 us)
Async XLA Ops:
  6.5 162.9 %all-reduce.2.cloned.1.call-start = ((), (), s32[]{:S(2)}) async-start(), calls=%async_computation.1 | async-start | bytes 524288 | tf_op jit(solution)/shard_map/psum | solution.py:71
  96.4 0.7 copy-start.1
  97.1 170.3 %reduce-scatter.2.cloned.1.call-start = ((), (), s32[]{:S(2)}) async-start(), calls=%async_computation.2 | async-start | bytes 294912 | tf_op jit(solution)/shard_map/reduce_scatter | solution.py:74
  204.9 0.7 copy-start
Sparse Core Ops, SparseCore 0:
  97.2 72.1 all-reduce.1
  205.7 61.6 reduce-scatter.1
where the time goes:
time: 277 us; the launch traced here: 276 us
  waiting for transfers between devices  112 us (40%)
  blocking collectives  75.3 us (27%)
  matrix products  25.4 us (9%)
  local copies, waits for them, and re-layouts  24 us (9%)
  loops' own time  17.1 us (6%)
  between operations  14.1 us (5%)
  other arithmetic  7.95 us (3%)
    reduce_scatter x1, waiting for transfers between devices, local(): mine = lax.psum_scatter(phi, ('ja', 'ka'), scatter_dimension=0, tiled=True)  61.8 us
    psum x1, waiting for transfers between devices, local(): totals = lax.psum(phi, ('ja', 'ka'))  49.9 us
    all_gather x1, blocking collectives, local(): whole = lax.all_gather(factor_a, ('ja', 'ka'), axis=0, tiled=True)  31.8 us
    dot_general x8, matrix products, add_block(): part = jnp.dot(ratio, panel, preferred_element_type=jnp.float32) * weight  24.7 us
    psum x1, blocking collectives, local(): mass = lax.psum(mass_part, ('ja', 'ka'))  21.7 us
    dynamic_slice x32, local copies, waits for them, and re-layouts, accumulate(): lax.scan(step, empty, (coords[:, 0], coords[:, 1], coords[:, 2], weights,...  21.4 us
    another operation x2, loops' own time, accumulate(): lax.scan(step, empty, (coords[:, 0], coords[:, 1], coords[:, 2], weights,...  17.1 us
    all_gather x1, blocking collectives, local(): rows_b = lax.all_gather(factor_b, 'ka', axis=0, tiled=True)  14.3 us
  transfers between devices with their start and end apart: 2, of which 2 were waited for; matrix products, arithmetic and copies ran while one was open for 0% of the time, Pallas kernels for 0%

commit v1 on v0

--- a/solution.py
+++ b/solution.py
@@ -68,7 +68,7 @@
 
     whole = lax.all_gather(factor_a, ("ja", "ka"), axis=0, tiled=True)
     phi = accumulate(whole.astype(jnp.bfloat16))
-    totals = lax.psum(phi, ("ja", "ka"))
+    totals = lax.psum(lax.psum(phi, "ka"), "ja")
     updated = whole * totals / mass_rows
     phi = accumulate(updated.astype(jnp.bfloat16))
     mine = lax.psum_scatter(phi, ("ja", "ka"), scatter_dimension=0, tiled=True)

time: 277 us -> 267 us (0.964)
  waiting for transfers between devices: 112 us -> 104 us
    psum x1 -> x2, waiting for transfers between devices: 49.9 us -> 41.2 us  [local(): totals = lax.psum(lax.psum(phi, 'ka'), 'ja')]
  transfers between devices with their start and end apart: 2 -> 3, of which waited for: 2 -> 3; matrix products, arithmetic and copies ran while one was open for 0% -> 0% of each run, Pallas kernels for 0% -> 0%
where the time goes in v1:
time: 267 us; the launch traced here: 266 us
  waiting for transfers between devices  104 us (39%)
  blocking collectives  74 us (28%)
  matrix products  25.4 us (10%)
  local copies, waits for them, and re-layouts  24 us (9%)
  loops' own time  17.1 us (6%)
  between operations  13.8 us (5%)
  other arithmetic  7.96 us (3%)
    reduce_scatter x1, waiting for transfers between devices, local(): mine = lax.psum_scatter(phi, ('ja', 'ka'), scatter_dimension=0, tiled=True)  62.6 us
    psum x2, waiting for transfers between devices, local(): totals = lax.psum(lax.psum(phi, 'ka'), 'ja')  41.2 us
    all_gather x1, blocking collectives, local(): whole = lax.all_gather(factor_a, ('ja', 'ka'), axis=0, tiled=True)  31.8 us
    dot_general x8, matrix products, add_block(): part = jnp.dot(ratio, panel, preferred_element_type=jnp.float32) * weight  24.8 us
    dynamic_slice x32, local copies, waits for them, and re-layouts, accumulate(): lax.scan(step, empty, (coords[:, 0], coords[:, 1], coords[:, 2], weights,...  21.4 us
    psum x1, blocking collectives, local(): mass = lax.psum(mass_part, ('ja', 'ka'))  20.4 us
    another operation x2, loops' own time, accumulate(): lax.scan(step, empty, (coords[:, 0], coords[:, 1], coords[:, 2], weights,...  17.1 us
    all_gather x1, blocking collectives, local(): rows_b = lax.all_gather(factor_b, 'ka', axis=0, tiled=True)  14.3 us
  transfers between devices with their start and end apart: 3, of which 3 were waited for; matrix products, arithmetic and copies ran while one was open for 0% of the time, Pallas kernels for 0%

profile of v1, /device:TPU:0, one launch (start us, length us, event | category | flops | bytes accessed | tf_op | source)
XLA Modules:
  0.0 266.3 jit_solution(2903980217069420917)
XLA Ops:
  6.5 0.8 copy.14
  7.5 7.5 %all_gather.11 = f32[256,256]{0,1:T(8,128)S(1)} all-gather(f32[256,64]{0,1:T(8,128)} %param.15), channel_id=1, replica_groups=mesh['ia'=4,'ja'=2,'ka'=4] {'ia'}, dimensions={1}, use_global_device_ids=true | all-gather | bytes 327680 | tf_op jit(solution)/shard_map/all_gather | solution.py:36
  15.1 14.3 %all_gather.10 = f32[256,256]{1,0:T(8,128)S(1)} all-gather(f32[64,256]{1,0:T(8,128)} %param.14), channel_id=1, replica_groups=mesh['ia'=4,'ja'=2,'ka'=4] {'ka'}, dimensions={0}, use_global_device_ids=true | all-gather | bytes 327680 | tf_op jit(solution)/shard_map/all_gather | solution.py:35
  30.1 31.8 %all_gather.9 = f32[256,256]{1,0:T(8,128)S(1)} all-gather(f32[32,256]{1,0:T(8,128)} %param.13), channel_id=1, replica_groups=mesh['ia'=4,'ja'=2,'ka'=4] {'ja','ka'}, dimensions={0}, use_global_device_ids=true | all-gather | bytes 294912 | tf_op jit(solution)/shard_map/all_gather | solution.py:69
  62.0 34.5 %while.20 = (s32[]{:T(128)}, f32[256,256]{1,0:T(8,128)S(1)}, s32[4]{0:T(128)S(1)}, s32[4,64,4096]{2,1,0:T(8,128)}, bf16[256,256]{1,0:T(8,128)(2,1)S(1)}, /*index...) while((s32[]{:T(128)}, f32[256,256]{1,0:T(8,128)S(1)}, ...), condition=%wide.region_1.0_spmd, body=%wide.region_0.0_spmd.sunk | while | flops 271351808 | bytes 7899463 | solution.py:64
  63.3 0.7 dynamic_slice.109
  64.7 0.7 multiply_convert_fusion.4
  65.4 0.7 dynamic_slice.107
  66.8 0.7 dynamic_slice.110
  67.5 3.1 %fusion.52 = f32[256,256]{1,0:T(8,128)S(1)} fusion(f32[256,256]{1,0:T(8,128)S(1)} %get-tuple-element.345, s32[]{:T(128)S(6)} %select_n.33, bf16[4096,256]{1,0:T(8,128)(2,1)S(1)} %bitcast.70, s32[4,64,4096]{2,1,0:T(8,128)} %get-tuple-element.361, s32[]{:T(128)} %get-tuple-element.344, f32[]{:T(128)} %bitcast.60, ...), kind=kOutput, calls=%fused_computation.6.clone.1 | convolution fusion | flops 269254656 | bytes 5408768 | tf_op jit(solution)/shard_map/while/body/eval_jaxpr/dot_general | solution.py:26
  71.9 0.7 dynamic_slice.109
  73.3 0.7 multiply_convert_fusion.4
  74.0 0.7 dynamic_slice.107
  75.4 0.7 dynamic_slice.110
  76.1 3.1 %fusion.52 = f32[256,256]{1,0:T(8,128)S(1)} fusion(f32[256,256]{1,0:T(8,128)S(1)} %get-tuple-element.345, s32[]{:T(128)S(6)} %select_n.33, bf16[4096,256]{1,0:T(8,128)(2,1)S(1)} %bitcast.70, s32[4,64,4096]{2,1,0:T(8,128)} %get-tuple-element.361, s32[]{:T(128)} %get-tuple-element.344, f32[]{:T(128)} %bitcast.60, ...), kind=kOutput, calls=%fused_computation.6.clone.1 | convolution fusion | flops 269254656 | bytes 5408768 | tf_op jit(solution)/shard_map/while/body/eval_jaxpr/dot_general | solution.py:26
  80.6 0.7 dynamic_slice.109
  82.0 0.7 multiply_convert_fusion.4
  82.6 0.7 dynamic_slice.107
  84.0 0.7 dynamic_slice.110
  84.7 3.1 %fusion.52 = f32[256,256]{1,0:T(8,128)S(1)} fusion(f32[256,256]{1,0:T(8,128)S(1)} %get-tuple-element.345, s32[]{:T(128)S(6)} %select_n.33, bf16[4096,256]{1,0:T(8,128)(2,1)S(1)} %bitcast.70, s32[4,64,4096]{2,1,0:T(8,128)} %get-tuple-element.361, s32[]{:T(128)} %get-tuple-element.344, f32[]{:T(128)} %bitcast.60, ...), kind=kOutput, calls=%fused_computation.6.clone.1 | convolution fusion | flops 269254656 | bytes 5408768 | tf_op jit(solution)/shard_map/while/body/eval_jaxpr/dot_general | solution.py:26
  89.2 0.7 dynamic_slice.109
  90.6 0.7 multiply_convert_fusion.4
  91.3 0.7 dynamic_slice.107
  92.6 0.7 dynamic_slice.110
  93.3 3.1 %fusion.52 = f32[256,256]{1,0:T(8,128)S(1)} fusion(f32[256,256]{1,0:T(8,128)S(1)} %get-tuple-element.345, s32[]{:T(128)S(6)} %select_n.33, bf16[4096,256]{1,0:T(8,128)(2,1)S(1)} %bitcast.70, s32[4,64,4096]{2,1,0:T(8,128)} %get-tuple-element.361, s32[]{:T(128)} %get-tuple-element.344, f32[]{:T(128)} %bitcast.60, ...), kind=kOutput, calls=%fused_computation.6.clone.1 | convolution fusion | flops 269254656 | bytes 5408768 | tf_op jit(solution)/shard_map/while/body/eval_jaxpr/dot_general | solution.py:26
  96.4 0.7 copy-done.1
  97.4 36.5 %all-reduce.3.cloned.1.call-done = f32[256,256]{1,0:T(8,128)} async-done(((f32[256,256]{1,0:T(8,128)}), f32[256,256]{1,0:T(8,128)}) %all-reduce.3.cloned.1.call-update) | async-done | bytes 262160 | tf_op jit(solution)/shard_map/psum | solution.py:71
  134.5 20.4 %psum.23 = f32[4,256]{1,0:T(4,128)S(1)} all-reduce(f32[4,256]{1,0:T(4,128)S(1)} %fusion.24), channel_id=1, replica_groups=mesh['ia'=4,'ja'=2,'ka'=4] {'ja','ka'}, use_global_device_ids=true, to_apply=%region_6.7 | all-reduce | flops 1024 | bytes 8192 | tf_op jit(solution)/shard_map/psum | solution.py:50
  154.9 4.6 %all-reduce.5.cloned.1.call-done = f32[256,256]{1,0:T(8,128)} async-done(((f32[256,256]{1,0:T(8,128)}), f32[256,256]{1,0:T(8,128)}) %all-reduce.5.cloned.1.call-update) | async-done | bytes 262160 | tf_op jit(solution)/shard_map/psum | solution.py:71
  159.5 1.0 fusion.33
  160.6 34.4 %while.21 = (s32[]{:T(128)}, f32[256,256]{1,0:T(8,128)S(1)}, s32[4]{0:T(128)S(1)}, s32[4,64,4096]{2,1,0:T(8,128)}, bf16[256,256]{1,0:T(8,128)(2,1)S(1)}, /*index...) while((s32[]{:T(128)}, f32[256,256]{1,0:T(8,128)S(1)}, ...), condition=%wide.region_8.9_spmd, body=%wide.region_7.8_spmd.sunk | while | flops 271351808 | bytes 7899463 | solution.py:64
  161.9 0.7 dynamic_slice.117
  163.3 0.7 multiply_convert_fusion.5
  164.0 0.7 dynamic_slice.115
  166.1 3.1 %fusion.56 = f32[256,256]{1,0:T(8,128)S(1)} fusion(f32[256,256]{1,0:T(8,128)S(1)} %get-tuple-element.387, s32[]{:T(128)S(6)} %select_n.36, bf16[4096,256]{1,0:T(8,128)(2,1)S(1)} %bitcast.71, s32[4,64,4096]{2,1,0:T(8,128)} %get-tuple-element.403, s32[]{:T(128)} %get-tuple-element.386, f32[]{:T(128)} %bitcast.68, ...), kind=kOutput, calls=%fused_computation.20.clone.1 | convolution fusion | flops 269254656 | bytes 5408768 | tf_op jit(solution)/shard_map/while/body/eval_jaxpr/dot_general | solution.py:26
  172.0 0.7 multiply_convert_fusion.5
  172.6 0.7 dynamic_slice.115
  174.7 3.1 %fusion.56 = f32[256,256]{1,0:T(8,128)S(1)} fusion(f32[256,256]{1,0:T(8,128)S(1)} %get-tuple-element.387, s32[]{:T(128)S(6)} %select_n.36, bf16[4096,256]{1,0:T(8,128)(2,1)S(1)} %bitcast.71, s32[4,64,4096]{2,1,0:T(8,128)} %get-tuple-element.403, s32[]{:T(128)} %get-tuple-element.386, f32[]{:T(128)} %bitcast.68, ...), kind=kOutput, calls=%fused_computation.20.clone.1 | convolution fusion | flops 269254656 | bytes 5408768 | tf_op jit(solution)/shard_map/while/body/eval_jaxpr/dot_general | solution.py:26
  179.2 0.7 dynamic_slice.117
  180.6 0.7 multiply_convert_fusion.5
  182.6 0.7 dynamic_slice.118
  183.3 3.1 %fusion.56 = f32[256,256]{1,0:T(8,128)S(1)} fusion(f32[256,256]{1,0:T(8,128)S(1)} %get-tuple-element.387, s32[]{:T(128)S(6)} %select_n.36, bf16[4096,256]{1,0:T(8,128)(2,1)S(1)} %bitcast.71, s32[4,64,4096]{2,1,0:T(8,128)} %get-tuple-element.403, s32[]{:T(128)} %get-tuple-element.386, f32[]{:T(128)} %bitcast.68, ...), kind=kOutput, calls=%fused_computation.20.clone.1 | convolution fusion | flops 269254656 | bytes 5408768 | tf_op jit(solution)/shard_map/while/body/eval_jaxpr/dot_general | solution.py:26
  187.8 0.7 dynamic_slice.117
  189.2 0.7 multiply_convert_fusion.5
  191.9 3.1 %fusion.56 = f32[256,256]{1,0:T(8,128)S(1)} fusion(f32[256,256]{1,0:T(8,128)S(1)} %get-tuple-element.387, s32[]{:T(128)S(6)} %select_n.36, bf16[4096,256]{1,0:T(8,128)(2,1)S(1)} %bitcast.71, s32[4,64,4096]{2,1,0:T(8,128)} %get-tuple-element.403, s32[]{:T(128)} %get-tuple-element.386, f32[]{:T(128)} %bitcast.68, ...), kind=kOutput, calls=%fused_computation.20.clone.1 | convolution fusion | flops 269254656 | bytes 5408768 | tf_op jit(solution)/shard_map/while/body/eval_jaxpr/dot_general | solution.py:26
  195.0 0.7 copy-done
  195.7 62.6 %reduce-scatter.2.cloned.1.call-done = f32[32,256]{1,0:T(8,128)} async-done(((f32[256,256]{1,0:T(8,128)}), f32[32,256]{1,0:T(8,128)}) %reduce-scatter.2.cloned.1.call-update) | async-done | bytes 32784 | tf_op jit(solution)/shard_map/reduce_scatter | solution.py:74
  258.3 1.4 dynamic-slice_divide_fusion
  (42 shorter events, 10.7 us)
Async XLA Ops:
  6.5 127.4 %all-reduce.3.cloned.1.call-start = ((), (), s32[]{:S(2)}) async-start(), calls=%async_computation.1 | async-start | bytes 524288 | tf_op jit(solution)/shard_map/psum | solution.py:71
  96.4 0.7 copy-start.1
  97.1 62.4 %all-reduce.5.cloned.1.call-start = ((), (), s32[]{:S(2)}) async-start(), calls=%async_computation.2 | async-start | bytes 524288 | tf_op jit(solution)/shard_map/psum | solution.py:71
  134.0 124.3 %reduce-scatter.2.cloned.1.call-start = ((), (), s32[]{:S(2)}) async-start(), calls=%async_computation.3 | async-start | bytes 294912 | tf_op jit(solution)/shard_map/reduce_scatter | solution.py:74
  195.0 0.7 copy-start
Sparse Core Ops, SparseCore 0:
  97.3 36.6 all-reduce.2
  136.2 23.2 all-reduce.4
  195.8 62.4 reduce-scatter.1
